TPU v7x, 32 devices: a whole 2x2x4 slice. The times are simulated.
32 devices in a mesh: grp: 4 (over x, core), dir: 8 (over z, y).
Axes of the slice: x: 2, y: 2, z: 4, core: 2. Of those that a mesh axis runs over, the one named last changes fastest.
Arguments:
- child_out: bfloat16 [512, 2, 8, 2048], P(('grp', 'dir')), may hold values from -6 to 6
- low_trans: bfloat16 [316, 2, 2048], replicated, may hold values from -0.59765625 to 0.59765625
- up_trans: bfloat16 [316, 2, 64, 128], P(None, None, 'dir'), may hold values from -0.41992188 to 0.41992188
- far_src: int32 [512, 96], P(('grp', 'dir')), may hold values from 0 to 15
- far_kind: int32 [512, 96], P(('grp', 'dir')), may hold values from 0 to 315
- far_len: int32 [512], P(('grp', 'dir')), may hold values from 1 to 96, as said below
- send_sel: int32 [4, 8, 8, 2], P('grp', 'dir'), may hold values from 0 to 15
- par_src: int32 [64, 96], P('grp'), may hold values from 0 to 31
- par_kind: int32 [64, 96], P('grp'), may hold values from 0 to 315
- par_len: int32 [64], P('grp'), may hold values from 1 to 96, as said below
- par_sel: int32 [4, 4, 8], replicated, may hold values from 0 to 15
Outputs:
- box_in: bfloat16 [512, 2, 8, 2048], P(('grp', 'dir'))
Inputs may be any that keep to these rules, and one draw needn't show every extreme that they name: Entries at positions from far_len[b] on are padding. Entries at positions from par_len[q] on are padding.
All inputs are finite; a program needn't handle non-finite values.
Results may differ from a plain program's by a relative error of at most 0.0052.
Values may be sent and summed in bfloat16 or wider, within the bound.
No kernel may reach another device: no remote copies, remote signals or barrier semaphores. Data moves between devices by JAX's collectives and lax.ppermute only.
A program may use at most 128 MiB of HBM per device.

v0:
```python
import functools
import math

import numpy as np

import jax
import jax.numpy as jnp
from jax import lax
from jax.experimental import pallas as pl
from jax.experimental.pallas import tpu as pltpu
from jax.sharding import PartitionSpec as P

TH1 = 32
PH1 = 64
TH2 = 64
PH2 = 128
WAVE_NUMBER = 2.5
LANES = 128


def interp_matrix(targets, sources):
    spacing = 2.0 * math.pi * (
        np.arange(targets)[:, None] / targets - np.arange(sources)[None, :] / sources
    )
    harmonics = np.arange(1, sources // 2)
    kernel = (
        1.0
        + 2.0 * np.sum(np.cos(spacing[:, :, None] * harmonics), axis=2)
        + np.cos(spacing * (sources // 2))
    )
    return kernel / sources


def phase_tables():
    polar = (np.arange(TH2) + 0.5) * (math.pi / TH2)
    azimuth = np.arange(PH2) * (2.0 * math.pi / PH2)
    along_x = np.sin(polar)[:, None] * np.cos(azimuth)[None, :]
    along_y = np.sin(polar)[:, None] * np.sin(azimuth)[None, :]
    along_z = np.cos(polar)[:, None] * np.ones((1, PH2))
    angles = []
    for c in range(4):
        sx, sy, sz = 2 * (c % 2) - 1, 2 * (c // 2 % 2) - 1, 2 * (c // 4 % 2) - 1
        angles.append(WAVE_NUMBER * (sx * along_x + sy * along_y + sz * along_z))
    angles = np.stack(angles)
    return np.cos(angles).astype(np.float32), np.sin(angles).astype(np.float32)


def vmem_call(kernel, out_shape, scratch, n_in, name):
    spec = pl.BlockSpec(memory_space=pltpu.VMEM)
    outs = jax.tree.map(lambda _: spec, out_shape)
    return pl.pallas_call(
        kernel,
        out_shape=out_shape,
        in_specs=[spec] * n_in,
        out_specs=outs,
        scratch_shapes=scratch,
        name=name,
    )


def aggregate_kernel(rhs, parents, x_ref, e1_ref, k1_ref, cos_ref, sin_ref, out_ref, w_ref):
    pairs = TH1 // 2

    def columns(j, carry):
        col = pl.multiple_of(j * LANES, LANES)
        wide = jnp.dot(
            x_ref[:, pl.ds(col, LANES)], e1_ref[...], preferred_element_type=jnp.float32
        )
        wide = wide.reshape(parents, 8, 2, rhs, 2, PH2)
        row = pl.multiple_of(j * 2 * rhs, 2 * rhs)
        for p in range(parents):
            for c in range(4):
                first, last = wide[p, c], wide[p, 7 - c]
                pieces = (
                    (0, 0, first[0] + last[0]),
                    (0, 1, first[1] + last[1]),
                    (1, 0, last[1] - first[1]),
                    (1, 1, first[0] - last[0]),
                )
                for which, half, value in pieces:
                    stacked = jnp.concatenate([value[:, 0], value[:, 1]], axis=0)
                    w_ref[p, c, which, pl.ds(row, 2 * rhs), half * PH2 : (half + 1) * PH2] = (
                        stacked.astype(jnp.bfloat16)
                    )
        return carry

    lax.fori_loop(0, pairs, columns, 0)
    dests = out_ref.shape[0]
    rows = TH2 // dests

    def one_parent(p, carry):
        total = None
        for c in range(4):
            for which, table in ((0, cos_ref), (1, sin_ref)):
                part = jnp.dot(k1_ref[...], w_ref[p, c, which], preferred_element_type=jnp.float32)
                factor = table[c]
                factor = jnp.concatenate([factor, factor], axis=1)[:, None, :]
                part = part.reshape(TH2, rhs, 2 * PH2) * factor
                total = part if total is None else total + part
        total = total.reshape(dests, rows * rhs, 2 * PH2).astype(jnp.bfloat16)
        for d in range(dests):
            out_ref[d, p] = total[d]
        return carry

    lax.fori_loop(0, parents, one_parent, 0)


def disaggregate_kernel(rhs, parents, z_ref, lower_ref, e2_ref, k2_ref, cos_ref, sin_ref, out_ref, l_ref):
    def one_parent(p, carry):
        dirs = z_ref.shape[0]
        z = jnp.concatenate([z_ref[d, p] for d in range(dirs)], axis=0).astype(jnp.float32)
        z = z.reshape(TH2, rhs, 2 * PH2)
        for c in range(4):
            narrow = []
            for table in (cos_ref, sin_ref):
                factor = table[c]
                factor = jnp.concatenate([factor, factor], axis=1)[:, None, :]
                turned = (z * factor).reshape(TH2 * rhs, 2 * PH2).astype(jnp.bfloat16)
                narrow.append(
                    jnp.dot(k2_ref[...], turned, preferred_element_type=jnp.float32)
                    .reshape(TH1, rhs, 2, PH2)
                )
            by_cos, by_sin = narrow
            for box, sign in ((c, 1.0), (7 - c, -1.0)):
                if sign > 0:
                    real = by_cos[:, :, 0] + by_sin[:, :, 1]
                    imag = by_cos[:, :, 1] - by_sin[:, :, 0]
                else:
                    real = by_cos[:, :, 0] - by_sin[:, :, 1]
                    imag = by_cos[:, :, 1] + by_sin[:, :, 0]
                both = jnp.concatenate([real, imag], axis=1).astype(jnp.bfloat16)
                row = pl.multiple_of((p * 8 + box) * 2 * rhs, 2 * rhs)
                for t in range(TH1):
                    half = t % 2
                    l_ref[t // 2, pl.ds(row, 2 * rhs), half * PH2 : (half + 1) * PH2] = both[t]
        return carry

    lax.fori_loop(0, parents, one_parent, 0)

    def columns(j, carry):
        col = pl.multiple_of(j * LANES, LANES)
        spread = jnp.dot(l_ref[j], e2_ref[...], preferred_element_type=jnp.float32)
        out_ref[:, pl.ds(col, LANES)] = (spread + lower_ref[:, pl.ds(col, LANES)]).astype(
            jnp.bfloat16
        )
        return carry

    lax.fori_loop(0, TH1 // 2, columns, 0)


def mix(w_ref, real_at, imag_at, target, first, count, column, imag_column, rhs):
    real = imag = None
    for i in range(count):
        row = first + i
        wr = w_ref[target, row : row + 1, pl.ds(column, LANES)]
        wi = w_ref[target, row : row + 1, pl.ds(imag_column, LANES)]
        wr = jnp.broadcast_to(wr, (rhs, LANES))
        wi = jnp.broadcast_to(wi, (rhs, LANES))
        re = wr * real_at[i] - wi * imag_at[i]
        im = wr * imag_at[i] + wi * real_at[i]
        real = re if real is None else real + re
        imag = im if imag is None else imag + im
    return real, imag


def lower_kernel(rhs, slots, w_ref, s_ref, out_ref):
    width = s_ref.shape[1]
    boxes = w_ref.shape[0]
    group = 16

    def columns(j, carry):
        col = pl.multiple_of(j * LANES, LANES)
        for base in range(0, slots, group):
            n = min(group, slots - base)
            block = s_ref[pl.ds(base * 2 * rhs, n * 2 * rhs), pl.ds(col, LANES)]
            block = block.astype(jnp.float32).reshape(n, 2, rhs, LANES)
            reals = [block[i, 0] for i in range(n)]
            imags = [block[i, 1] for i in range(n)]

            def one_box(b, inner):
                real, imag = mix(
                    w_ref, reals, imags, b, base, n, col, width + col, rhs
                )
                both = jnp.concatenate([real, imag], axis=0)
                row = pl.multiple_of(b * 2 * rhs, 2 * rhs)
                place = (pl.ds(row, 2 * rhs), pl.ds(col, LANES))
                if base:
                    both = both + out_ref[place]
                out_ref[place] = both
                return inner

            lax.fori_loop(0, boxes, one_box, 0)
        return carry

    lax.fori_loop(0, width // LANES, columns, 0)


def parent_kernel(rhs, slots, w_ref, s_ref, out_ref, acc_ref):
    rows = s_ref.shape[1] // rhs
    targets = w_ref.shape[0]
    group = 16

    def two_rows(j, carry):
        first = pl.multiple_of(j * 2 * rhs, 2 * rhs)
        for step in range(2):
            column = pl.multiple_of((j * 2 + step) * LANES, LANES)
            imag_column = column + rows * LANES
            for base in range(0, slots, group):
                n = min(group, slots - base)
                reals, imags = [], []
                for i in range(n):
                    block = s_ref[base + i, pl.ds(first, 2 * rhs), :].astype(jnp.float32)
                    block = block[step * rhs : (step + 1) * rhs]
                    reals.append(block[:, :LANES])
                    imags.append(block[:, LANES:])

                def one_target(q, inner):
                    real, imag = mix(
                        w_ref, reals, imags, q, base, n, column, imag_column, rhs
                    )
                    if base:
                        real = real + acc_ref[q, step, :, :LANES]
                        imag = imag + acc_ref[q, step, :, LANES:]
                    acc_ref[q, step, :, :LANES] = real
                    acc_ref[q, step, :, LANES:] = imag
                    return inner

                lax.fori_loop(0, targets, one_target, 0)

        def pack(q, inner):
            both = jnp.concatenate([acc_ref[q, 0], acc_ref[q, 1]], axis=0)
            out_ref[q, pl.ds(first, 2 * rhs), :] = both.astype(jnp.bfloat16)
            return inner

        lax.fori_loop(0, targets, pack, 0)
        return carry

    lax.fori_loop(0, rows // 2, two_rows, 0)


def pair_counts(source_index, kind_index, lengths, slot_count, kind_count):
    entries = source_index.shape[1]
    live = jnp.arange(entries, dtype=jnp.int32)[None, :] < lengths[:, None]
    slot_ids = jnp.arange(slot_count, dtype=jnp.int32)
    kind_ids = jnp.arange(kind_count, dtype=jnp.int32)
    hit_slot = ((source_index[:, :, None] == slot_ids) & live[:, :, None]).astype(jnp.bfloat16)
    hit_kind = (kind_index[:, :, None] == kind_ids).astype(jnp.bfloat16)
    counts = jnp.einsum("bjs,bjk->bsk", hit_slot, hit_kind, preferred_element_type=jnp.float32)
    return counts.astype(jnp.bfloat16).reshape(-1, kind_count)


def body(
    child_out,
    low_trans,
    up_trans,
    far_src,
    far_kind,
    far_len,
    send_sel,
    par_src,
    par_kind,
    par_len,
    par_sel,
):
    boxes_here, _, rhs, width = child_out.shape
    parents_here = boxes_here // 8
    dirs = lax.axis_size("dir")
    groups = lax.axis_size("grp")
    group_index = lax.axis_index("grp")
    kinds = low_trans.shape[0]
    rows_here = TH2 // dirs
    tall = 2 * PH2

    rows_up, cols_up = interp_matrix(TH2, TH1), interp_matrix(PH2, PH1)
    scale = TH1 / TH2 * (PH1 / PH2)
    bf = lambda a: jnp.asarray(a.astype(np.float32)).astype(jnp.bfloat16)
    e1 = bf(np.kron(np.eye(2), cols_up.T))
    k1 = bf(np.kron(rows_up, np.eye(rhs)))
    e2 = bf(np.kron(np.eye(2), cols_up) * scale)
    k2 = bf(np.kron(rows_up.T, np.eye(rhs)))
    cosine, sine = phase_tables()
    cosine, sine = jnp.asarray(cosine), jnp.asarray(sine)

    outgoing = child_out[send_sel[0, 0]]
    arrived = lax.all_to_all(outgoing, "dir", split_axis=0, concat_axis=0, tiled=True)
    low_slots = dirs * send_sel.shape[3]

    flat = child_out.reshape(boxes_here * 2 * rhs, width)
    parent_out = vmem_call(
        functools.partial(aggregate_kernel, rhs, parents_here),
        jax.ShapeDtypeStruct((dirs, parents_here, rows_here * rhs, tall), jnp.bfloat16),
        [pltpu.VMEM((parents_here, 4, 2, TH1 * rhs, tall), jnp.bfloat16)],
        5,
        "aggregate",
    )(flat, e1, k1, cosine, sine)
    sliced = lax.all_to_all(parent_out, "dir", split_axis=0, concat_axis=0, tiled=True)
    sliced = sliced.reshape((dirs * parents_here,) + sliced.shape[2:])
    offered = sliced[par_sel[group_index]]
    candidates = lax.all_to_all(offered, "grp", split_axis=0, concat_axis=0, tiled=True)
    up_slots = groups * par_sel.shape[2]
    candidates = candidates.reshape((up_slots,) + candidates.shape[2:])

    up_counts = pair_counts(par_src, par_kind, par_len, up_slots, kinds)
    up_weights = jnp.dot(
        up_counts, up_trans.reshape(kinds, -1), preferred_element_type=jnp.float32
    )
    targets = par_src.shape[0]
    parent_in = vmem_call(
        functools.partial(parent_kernel, rhs, up_slots),
        jax.ShapeDtypeStruct((targets, rows_here * rhs, tall), jnp.bfloat16),
        [pltpu.VMEM((targets, 2, rhs, tall), jnp.float32)],
        2,
        "parent_far",
    )(up_weights.reshape(targets, up_slots, -1), candidates)
    parent_in = parent_in.reshape(dirs, parents_here, rows_here * rhs, tall)
    returned = lax.all_to_all(parent_in, "dir", split_axis=0, concat_axis=0, tiled=True)

    low_counts = pair_counts(far_src, far_kind, far_len, low_slots, kinds)
    low_weights = jnp.dot(
        low_counts, low_trans.reshape(kinds, -1), preferred_element_type=jnp.float32
    )
    lower = vmem_call(
        functools.partial(lower_kernel, rhs, low_slots),
        jax.ShapeDtypeStruct((boxes_here * 2 * rhs, width), jnp.float32),
        [],
        2,
        "lower_far",
    )(low_weights.reshape(boxes_here, low_slots, -1), arrived.reshape(low_slots * 2 * rhs, width))

    out = vmem_call(
        functools.partial(disaggregate_kernel, rhs, parents_here),
        jax.ShapeDtypeStruct((boxes_here * 2 * rhs, width), jnp.bfloat16),
        [pltpu.VMEM((TH1 // 2, boxes_here * 2 * rhs, 2 * PH2), jnp.bfloat16)],
        6,
        "disaggregate",
    )(returned, lower, e2, k2, cosine, sine)
    return out.reshape(child_out.shape)


def solution(mesh):
    in_specs = (
        P(("grp", "dir"), None, None, None),
        P(),
        P(None, None, "dir", None),
        P(("grp", "dir"), None),
        P(("grp", "dir"), None),
        P(("grp", "dir")),
        P("grp", "dir", None, None),
        P("grp", None),
        P("grp", None),
        P("grp"),
        P(),
    )
    out_specs = P(("grp", "dir"), None, None, None)
    return jax.shard_map(body, mesh=mesh, in_specs=in_specs, out_specs=out_specs, check_vma=False)
```

profile of v0, /device:TPU:0, one launch (start us, length us, event | category | flops | bytes accessed | tf_op | source)
XLA Modules:
  0.0 120.1 jit_solution(7005795138819181783)
XLA Ops:
  0.0 9.8 %aggregate.1 = bf16[8,2,64,256]{3,2,1,0:T(8,128)(2,1)} custom-call(bf16[256,2048]{1,0:T(8,128)(2,1)} %bitcast.22, bf16[128,256]{1,0:T(8,128)(2,1)} %constant.37.e1_ref, bf16[512,256]{1,0:T(8,128)(2,1)} %constant.38.k1_ref, f32[4,64,128]{2,1,0:T(8,128)} %constant.30.clone.cos_ref, f32[4,64,128]{2,1,0:T(8,128)} %constant.31.clone.sin_ref), custom_call_target="tpu_custom_call" | custom-call | tf_op jit(solution)/shard_map/aggregate/pallas_call | solution.py:289
  9.8 7.3 %all-to-all-start = ((bf16[8,2,64,256]{3,2,1,0:T(8,128)(2,1)}), bf16[8,2,64,256]{3,2,1,0:T(8,128)(2,1)S(1)}, u32[]{:S(2)}, u32[]{:S(2)}) async-start(bf16[8,2,64,256]{3,2,1,0:T(8,128)(2,1)} %aggregate.1), calls=%async_computation | async-start | bytes 1048576 | tf_op jit(solution)/shard_map/all_to_all | solution.py:296
  17.1 0.0 copy-start.1
  17.1 0.8 compare_select_fusion
  17.9 0.1 reshape.144
  18.0 13.6 %all-to-all-done = bf16[8,2,64,256]{3,2,1,0:T(8,128)(2,1)S(1)} async-done(((bf16[8,2,64,256]{3,2,1,0:T(8,128)(2,1)}), bf16[8,2,64,256]{3,2,1,0:T(8,128)(2,1)S(1)}, u32[]{:S(2)}, u32[]{:S(2)}) %all-to-all-start) | async-done | bytes 524320 | tf_op jit(solution)/shard_map/all_to_all | solution.py:296
  31.6 1.6 %gather_fusion = bf16[32,64,256]{2,1,0:T(8,128)(2,1)} fusion(bf16[16,64,256]{2,1,0:T(8,128)(2,1)S(1)} %bitcast.20, s32[1024]{0:T(1024)S(1)} %pad_clamp_fusion.1), kind=kCustom, calls=%fused_computation | custom fusion | bytes 2097280 | tf_op jit(solution)/shard_map/gather | solution.py:298
  33.2 3.5 %all-to-all-start.1 = ((bf16[4,8,64,256]{3,2,1,0:T(8,128)(2,1)}), bf16[4,8,64,256]{3,2,1,0:T(8,128)(2,1)S(1)}, u32[]{:S(2)}, u32[]{:S(2)}) async-start(bf16[4,8,64,256]{3,2,1,0:T(8,128)(2,1)} %bitcast.3), calls=%async_computation.1 | async-start | bytes 2097152 | tf_op jit(solution)/shard_map/all_to_all | solution.py:299
  36.7 0.0 copy-done.8
  36.7 0.1 copy.19
  36.8 0.1 reshape.152
  36.9 0.0 copy-done.1
  36.9 1.6 %gather_fusion.1 = bf16[16,2,8,2048]{3,2,1,0:T(8,128)(2,1)} fusion(bf16[16,2,8,2048]{3,2,1,0:T(8,128)(2,1)S(1)} %copy-done.1, s32[1024]{0:T(1024)S(1)} %pad_clamp_fusion), kind=kCustom, calls=%fused_computation.1 | custom fusion | bytes 2097216 | tf_op jit(solution)/shard_map/gather | solution.py:284
  38.5 12.6 %all-to-all-done.1 = bf16[4,8,64,256]{3,2,1,0:T(8,128)(2,1)S(1)} async-done(((bf16[4,8,64,256]{3,2,1,0:T(8,128)(2,1)}), bf16[4,8,64,256]{3,2,1,0:T(8,128)(2,1)S(1)}, u32[]{:S(2)}, u32[]{:S(2)}) %all-to-all-start.1) | async-done | bytes 1048608 | tf_op jit(solution)/shard_map/all_to_all | solution.py:299
  51.1 3.6 %all-to-all-start.3 = ((bf16[8,2,2,8,2048]{4,3,2,1,0:T(8,128)(2,1)}), bf16[8,2,2,8,2048]{4,3,2,1,0:T(8,128)(2,1)S(1)}, u32[]{:S(2)}, u32[]{:S(2)}) async-start(bf16[8,2,2,8,2048]{4,3,2,1,0:T(8,128)(2,1)} %bitcast.7), calls=%async_computation.3 | async-start | bytes 2097152 | tf_op jit(solution)/shard_map/all_to_all | solution.py:285
  54.8 2.4 %reshape.160 = bf16[316,2048,1]{1,0,2:T(8,128)(2,1)S(1)} reshape(bf16[316,2,8,128]{3,2,1,0:T(8,128)(2,1)} %param.19) | data formatting | bytes 2588672 | tf_op jit(solution)/shard_map/reshape | solution.py:305
  57.1 0.0 copy-done.9
  57.1 0.1 iota_compare_fusion.15
  57.2 3.8 %fusion.3.w_ref = f32[16,32,2048]{2,1,0:T(8,128)} fusion(bf16[316,2048,1]{1,0,2:T(8,128)(2,1)S(1)} %reshape.160, s32[16,96]{1,0:T(8,128)S(1)} %copy-done.4, s32[16,96]{1,0:T(8,128)S(1)} %copy-done.5, pred[16,96]{1,0:T(8,128)(4,1)S(1)} %iota_compare_fusion.15), kind=kOutput, calls=%fused_computation.7 | convolution fusion | flops 694509568 | bytes 5502464 | tf_op jit(solution)/shard_map/dot_general | solution.py:304
  61.0 11.6 %parent_far.1 = bf16[16,64,256]{2,1,0:T(8,128)(2,1)} custom-call(f32[16,32,2048]{2,1,0:T(8,128)} %fusion.3.w_ref, bf16[32,64,256]{2,1,0:T(8,128)(2,1)} %bitcast.23), custom_call_target="tpu_custom_call" | custom-call | tf_op jit(solution)/shard_map/parent_far/pallas_call | solution.py:308
  72.6 7.7 %all-to-all-done.3 = bf16[8,2,2,8,2048]{4,3,2,1,0:T(8,128)(2,1)S(1)} async-done(((bf16[8,2,2,8,2048]{4,3,2,1,0:T(8,128)(2,1)}), bf16[8,2,2,8,2048]{4,3,2,1,0:T(8,128)(2,1)S(1)}, u32[]{:S(2)}, u32[]{:S(2)}) %all-to-all-start.3) | async-done | bytes 1048608 | tf_op jit(solution)/shard_map/all_to_all | solution.py:285
  80.4 1.0 copy-done
  81.4 3.5 %all-to-all-start.2 = ((bf16[8,2,64,256]{3,2,1,0:T(8,128)(2,1)}), bf16[8,2,64,256]{3,2,1,0:T(8,128)(2,1)S(1)}, u32[]{:S(2)}, u32[]{:S(2)}) async-start(bf16[8,2,64,256]{3,2,1,0:T(8,128)(2,1)} %bitcast.24), calls=%async_computation.2 | async-start | bytes 1048576 | tf_op jit(solution)/shard_map/all_to_all | solution.py:316
  84.9 0.0 copy-start.6
  84.9 0.0 copy-start.7
  84.9 6.0 %reshape.161 = bf16[316,4096,1]{1,0,2:T(8,128)(2,1)S(1)} reshape(bf16[316,2,2048]{2,1,0:T(2,128)(2,1)} %param.18) | data formatting | bytes 5177344 | tf_op jit(solution)/shard_map/reshape | solution.py:320
  90.9 0.1 iota_compare_fusion.14
  91.0 4.1 %fusion.8.w_ref = f32[16,16,4096]{2,1,0:T(8,128)} fusion(bf16[316,4096,1]{1,0,2:T(8,128)(2,1)S(1)} %reshape.161, s32[16,96]{1,0:T(8,128)S(1)} %copy-done.6, s32[16,96]{1,0:T(8,128)S(1)} %copy-done.7, pred[16,96]{1,0:T(8,128)(4,1)S(1)} %iota_compare_fusion.14), kind=kOutput, calls=%fused_computation.11 | convolution fusion | flops 678847488 | bytes 6796800 | tf_op jit(solution)/shard_map/dot_general | solution.py:319
  95.2 12.3 %lower_far.1.lower_ref = f32[256,2048]{1,0:T(8,128)} custom-call(f32[16,16,4096]{2,1,0:T(8,128)} %fusion.8.w_ref, bf16[256,2048]{1,0:T(8,128)(2,1)} %bitcast.21), custom_call_target="tpu_custom_call" | custom-call | tf_op jit(solution)/shard_map/lower_far/pallas_call | solution.py:322
  107.5 0.0 all-to-all-done.2.z_ref
  107.5 0.8 copy-done.3
  108.3 11.8 %disaggregate.1 = bf16[256,2048]{1,0:T(8,128)(2,1)} custom-call(bf16[8,2,64,256]{3,2,1,0:T(8,128)(2,1)} %copy-done.3, f32[256,2048]{1,0:T(8,128)} %lower_far.1.lower_ref, bf16[256,128]{1,0:T(8,128)(2,1)} %constant.39.e2_ref, bf16[256,512]{1,0:T(8,128)(2,1)} %constant.40.k2_ref, f32[4,64,128]{2,1,0:T(8,128)} %constant.30.clone.cos_ref, ...), custom_call_target="tpu_custom_call" | custom-call | tf_op jit(solution)/shard_map/disaggregate/pallas_call | solution.py:330
  (17 shorter events, 0.0 us)
Async XLA Ops:
  9.8 21.8 %all-to-all-start = ((bf16[8,2,64,256]{3,2,1,0:T(8,128)(2,1)}), bf16[8,2,64,256]{3,2,1,0:T(8,128)(2,1)S(1)}, u32[]{:S(2)}, u32[]{:S(2)}) async-start(bf16[8,2,64,256]{3,2,1,0:T(8,128)(2,1)} %aggregate.1), calls=%async_computation | async-start | bytes 1048576 | tf_op jit(solution)/shard_map/all_to_all | solution.py:296
  17.1 19.6 %copy-start.8 = (s32[1,1,8,2]{2,3,1,0:T(2,128)S(1)}, s32[1,1,8,2]{2,3,1,0:T(2,128)}, u32[]{:S(2)}) copy-start(s32[1,1,8,2]{2,3,1,0:T(2,128)} %param.23) | copy-start | bytes 196
  17.1 19.8 %copy-start.1 = (bf16[16,2,8,2048]{3,2,1,0:T(8,128)(2,1)S(1)}, bf16[16,2,8,2048]{3,2,1,0:T(8,128)(2,1)}, u32[]{:S(2)}) copy-start(bf16[16,2,8,2048]{3,2,1,0:T(8,128)(2,1)} %param.17) | copy-start | bytes 3145732
  33.2 17.9 %all-to-all-start.1 = ((bf16[4,8,64,256]{3,2,1,0:T(8,128)(2,1)}), bf16[4,8,64,256]{3,2,1,0:T(8,128)(2,1)S(1)}, u32[]{:S(2)}, u32[]{:S(2)}) async-start(bf16[4,8,64,256]{3,2,1,0:T(8,128)(2,1)} %bitcast.3), calls=%async_computation.1 | async-start | bytes 2097152 | tf_op jit(solution)/shard_map/all_to_all | solution.py:299
  38.5 18.6 %copy-start.9 = (s32[16]{0:T(128)S(1)}, s32[16]{0:T(128)}, u32[]{:S(2)}) copy-start(s32[16]{0:T(128)} %param.26) | copy-start | bytes 196
  38.5 18.7 %copy-start.4 = (s32[16,96]{1,0:T(8,128)S(1)}, s32[16,96]{1,0:T(8,128)}, u32[]{:S(2)}) copy-start(s32[16,96]{1,0:T(8,128)} %param.25) | copy-start | bytes 18436
  38.5 18.7 %copy-start.5 = (s32[16,96]{1,0:T(8,128)S(1)}, s32[16,96]{1,0:T(8,128)}, u32[]{:S(2)}) copy-start(s32[16,96]{1,0:T(8,128)} %param.24) | copy-start | bytes 18436
  51.1 9.9 %copy-start.2 = (bf16[4,8,64,256]{3,2,1,0:T(8,128)(2,1)}, bf16[4,8,64,256]{3,2,1,0:T(8,128)(2,1)S(1)}, u32[]{:S(2)}) copy-start(bf16[4,8,64,256]{3,2,1,0:T(8,128)(2,1)S(1)} %all-to-all-done.1) | copy-start | bytes 3145732
  51.1 29.3 %all-to-all-start.3 = ((bf16[8,2,2,8,2048]{4,3,2,1,0:T(8,128)(2,1)}), bf16[8,2,2,8,2048]{4,3,2,1,0:T(8,128)(2,1)S(1)}, u32[]{:S(2)}, u32[]{:S(2)}) async-start(bf16[8,2,2,8,2048]{4,3,2,1,0:T(8,128)(2,1)} %bitcast.7), calls=%async_computation.3 | async-start | bytes 2097152 | tf_op jit(solution)/shard_map/all_to_all | solution.py:285
  80.4 1.0 copy-start
  81.4 26.2 %all-to-all-start.2 = ((bf16[8,2,64,256]{3,2,1,0:T(8,128)(2,1)}), bf16[8,2,64,256]{3,2,1,0:T(8,128)(2,1)S(1)}, u32[]{:S(2)}, u32[]{:S(2)}) async-start(bf16[8,2,64,256]{3,2,1,0:T(8,128)(2,1)} %bitcast.24), calls=%async_computation.2 | async-start | bytes 1048576 | tf_op jit(solution)/shard_map/all_to_all | solution.py:316
  84.9 6.0 %copy-start.10 = (s32[16]{0:T(128)S(1)}, s32[16]{0:T(128)}, u32[]{:S(2)}) copy-start(s32[16]{0:T(128)} %param.22) | copy-start | bytes 196
  84.9 6.1 %copy-start.6 = (s32[16,96]{1,0:T(8,128)S(1)}, s32[16,96]{1,0:T(8,128)}, u32[]{:S(2)}) copy-start(s32[16,96]{1,0:T(8,128)} %param.21) | copy-start | bytes 18436
  84.9 6.1 %copy-start.7 = (s32[16,96]{1,0:T(8,128)S(1)}, s32[16,96]{1,0:T(8,128)}, u32[]{:S(2)}) copy-start(s32[16,96]{1,0:T(8,128)} %param.20) | copy-start | bytes 18436
  107.5 0.8 copy-start.3
where the time goes:
time: 121 us; the launch traced here: 120 us
  Pallas kernels  45.6 us (38%)
  waiting for transfers between devices  33.9 us (28%)
  starting transfers between devices  18 us (15%)
  local copies, waits for them, and re-layouts  13.6 us (11%)
  matrix products  7.93 us (7%)
    all_to_all x1, waiting for transfers between devices, body(): lax.all_to_all(parent_out, 'dir', split_axis=0, concat_axis=0, tiled=True)  13.6 us
    all_to_all x1, waiting for transfers between devices, body(): lax.all_to_all(offered, 'grp', split_axis=0, concat_axis=0, tiled=True)  12.6 us
    pallas_call x1, Pallas kernels, body(): vmem_call(functools.partial(lower_kernel, rhs, low_slots), jax.ShapeDtype...  12.3 us
    pallas_call x1, Pallas kernels, body(): vmem_call(functools.partial(disaggregate_kernel, rhs, parents_here), jax....  11.8 us
    pallas_call x1, Pallas kernels, body(): vmem_call(functools.partial(parent_kernel, rhs, up_slots), jax.ShapeDtype...  11.6 us
    pallas_call x1, Pallas kernels, body(): vmem_call(functools.partial(aggregate_kernel, rhs, parents_here), jax.Sha...  9.81 us
    all_to_all x1, waiting for transfers between devices, body(): lax.all_to_all(outgoing, 'dir', split_axis=0, concat_axis=0, tiled=True)  7.75 us
    all_to_all x1, starting transfers between devices, body(): lax.all_to_all(parent_out, 'dir', split_axis=0, concat_axis=0, tiled=True)  7.31 us
  transfers between devices with their start and end apart: 4, of which 3 were waited for; matrix products, arithmetic and copies ran while one was open for 16% of the time, Pallas kernels for 20%

commit v1 on v0

v1 whole, which is shorter than its diff:
```python
import functools
import math

import numpy as np

import jax
import jax.numpy as jnp
from jax import lax
from jax.experimental import pallas as pl
from jax.experimental.pallas import tpu as pltpu
from jax.sharding import PartitionSpec as P


TH1 = 32
PH1 = 64
TH2 = 64
PH2 = 128
WAVE_NUMBER = 2.5
LANES = 128
VMEM_LIMIT = 20 << 20


def interp_matrix(targets, sources):
    spacing = 2.0 * math.pi * (
        np.arange(targets)[:, None] / targets - np.arange(sources)[None, :] / sources
    )
    harmonics = np.arange(1, sources // 2)
    kernel = (
        1.0
        + 2.0 * np.sum(np.cos(spacing[:, :, None] * harmonics), axis=2)
        + np.cos(spacing * (sources // 2))
    )
    return kernel / sources


def phase_tables():
    polar = (np.arange(TH2) + 0.5) * (math.pi / TH2)
    azimuth = np.arange(PH2) * (2.0 * math.pi / PH2)
    along_x = np.sin(polar)[:, None] * np.cos(azimuth)[None, :]
    along_y = np.sin(polar)[:, None] * np.sin(azimuth)[None, :]
    along_z = np.cos(polar)[:, None] * np.ones((1, PH2))
    angles = []
    for c in range(4):
        sx, sy, sz = 2 * (c % 2) - 1, 2 * (c // 2 % 2) - 1, 2 * (c // 4 % 2) - 1
        angles.append(WAVE_NUMBER * (sx * along_x + sy * along_y + sz * along_z))
    angles = np.stack(angles)
    return np.cos(angles).astype(np.float32), np.sin(angles).astype(np.float32)


def vmem_call(kernel, out_shape, scratch, n_in, n_smem=0):
    spec = pl.BlockSpec(memory_space=pltpu.VMEM)
    outs = jax.tree.map(lambda _: spec, out_shape)
    return pl.pallas_call(
        kernel,
        out_shape=out_shape,
        in_specs=[pl.BlockSpec(memory_space=pltpu.SMEM)] * n_smem + [spec] * n_in,
        out_specs=outs,
        scratch_shapes=scratch,
        compiler_params=pltpu.CompilerParams(vmem_limit_bytes=VMEM_LIMIT),
    )


def select_kernel(send_ref, x_ref, *outs):
    place = lax.axis_index("dir")
    for k, out_ref in enumerate(outs):
        for i in range(out_ref.shape[0]):
            out_ref[i] = x_ref[send_ref[place ^ k, i]]


def weights_kernel(slots, axis, each, length_ref, source_ref, kind_ref, table_ref, out_ref, count_ref):
    targets, entries = source_ref.shape
    kinds = table_ref.shape[0]
    order = lax.broadcasted_iota(jnp.int32, (slots, entries), 0)
    slot_ids = ((order // each) ^ lax.axis_index(axis)) * each + order % each
    kind_ids = lax.broadcasted_iota(jnp.int32, (kinds, entries), 0)
    places = lax.broadcasted_iota(jnp.int32, (slots, entries), 1)
    for b in range(targets):
        source = jnp.broadcast_to(source_ref[b : b + 1, :], (slots, entries))
        kind = jnp.broadcast_to(kind_ref[b : b + 1, :], (kinds, entries))
        hit = (source == slot_ids) & (places < length_ref[b])
        hit_slot = jnp.where(hit, 1.0, 0.0).astype(jnp.bfloat16)
        hit_kind = jnp.where(kind == kind_ids, 1.0, 0.0).astype(jnp.bfloat16)
        counts = lax.dot_general(
            hit_slot, hit_kind, (((1,), (1,)), ((), ())), preferred_element_type=jnp.float32
        )
        count_ref[b * slots : (b + 1) * slots, :] = counts.astype(jnp.bfloat16)
    tile = 2 * LANES

    def columns(j, carry):
        place = rows_of(j, tile)
        value = jnp.dot(count_ref[...], table_ref[:, place], preferred_element_type=jnp.float32)
        out_ref[:, :, place] = value.reshape(targets, slots, tile)
        return carry

    lax.fori_loop(0, table_ref.shape[1] // tile, columns, 0)


def rows_of(index, size):
    return pl.ds(pl.multiple_of(index * size, size), size)


def aggregate_kernel(rhs, parents, dirs, x_ref, e1_ref, k1_ref, cos_ref, sin_ref, *refs):
    out_ref, w_ref, acc_ref = refs

    def columns(j, carry):
        wide = jnp.dot(
            x_ref[:, rows_of(j, LANES)], e1_ref[...], preferred_element_type=jnp.float32
        )
        place = rows_of(j, 2 * rhs)
        for p in range(parents):
            for c in range(4):
                first, last = (p * 8 + c) * 2 * rhs, (p * 8 + 7 - c) * 2 * rhs
                pick = lambda row, part: wide[row + part * rhs : row + (part + 1) * rhs]
                pieces = (
                    (0, 0, pick(first, 0) + pick(last, 0)),
                    (0, 1, pick(first, 1) + pick(last, 1)),
                    (1, 0, pick(last, 1) - pick(first, 1)),
                    (1, 1, pick(first, 0) - pick(last, 0)),
                )
                for which, half, value in pieces:
                    stacked = jnp.concatenate([value[:, :PH2], value[:, PH2:]], axis=0)
                    w_ref[p, c, which, place, half * PH2 : (half + 1) * PH2] = stacked.astype(
                        jnp.bfloat16
                    )
        return carry

    lax.fori_loop(0, TH1 // 2, columns, 0)

    def one_parent(p, carry):
        for c in range(4):
            parts = [
                jnp.dot(k1_ref[...], w_ref[p, c, which], preferred_element_type=jnp.float32)
                for which in range(2)
            ]
            for s in range(TH2):
                rows = slice(s * rhs, (s + 1) * rhs)
                fc = jnp.broadcast_to(cos_ref[c, s : s + 1, :], (rhs, PH2))
                fs = jnp.broadcast_to(sin_ref[c, s : s + 1, :], (rhs, PH2))
                for half in range(2):
                    lanes = slice(half * PH2, (half + 1) * PH2)
                    value = parts[0][rows, lanes] * fc + parts[1][rows, lanes] * fs
                    if c:
                        value = value + acc_ref[rows, lanes]
                    acc_ref[rows, lanes] = value
        size = TH2 // dirs * rhs
        for k in range(dirs):
            out_ref[k, p] = acc_ref[k * size : (k + 1) * size, :].astype(jnp.bfloat16)
        return carry

    lax.fori_loop(0, parents, one_parent, 0)


def offer_kernel(pick_ref, in_ref, *outs):
    group = lax.axis_index("grp")
    for k, out_ref in enumerate(outs):
        for i in range(out_ref.shape[0]):
            out_ref[i] = in_ref[pick_ref[group, group ^ k, i]]


def disaggregate_kernel(
    rhs, in_ref, lower_ref, e2_ref, k2_ref, cos_ref, sin_ref, out_ref, z_ref, turn_ref, l_ref
):
    dirs, parents, size, _ = in_ref.shape
    for k in range(dirs):
        for p in range(parents):
            z_ref[p, k * size : (k + 1) * size, :] = in_ref[k, p].astype(jnp.float32)

    def one_parent(p, carry):
        for c in range(4):
            for s in range(0, TH2, 2):
                rows = slice(s * rhs, (s + 2) * rhs)
                for which, table in ((0, cos_ref), (1, sin_ref)):
                    factor = [
                        jnp.broadcast_to(table[c, s + i : s + i + 1, :], (rhs, PH2))
                        for i in range(2)
                    ]
                    factor = jnp.concatenate(factor, axis=0)
                    for half in range(2):
                        lanes = slice(half * PH2, (half + 1) * PH2)
                        turn_ref[which, rows, lanes] = (z_ref[p, rows, lanes] * factor).astype(
                            jnp.bfloat16
                        )
            by_cos, by_sin = [
                jnp.dot(k2_ref[...], turn_ref[which], preferred_element_type=jnp.float32)
                for which in range(2)
            ]
            cr, ci = by_cos[:, :PH2], by_cos[:, PH2:]
            sr, si = by_sin[:, :PH2], by_sin[:, PH2:]
            for box, real, imag in ((c, cr + si, ci - sr), (7 - c, cr - si, ci + sr)):
                place = rows_of(p * 8 + box, 2 * rhs)
                for t in range(TH1):
                    rows = slice(t * rhs, (t + 1) * rhs)
                    both = jnp.concatenate([real[rows], imag[rows]], axis=0)
                    half = t % 2
                    l_ref[t // 2, place, half * PH2 : (half + 1) * PH2] = both.astype(jnp.bfloat16)
        return carry

    lax.fori_loop(0, parents, one_parent, 0)

    def columns(j, carry):
        place = rows_of(j, LANES)
        spread = jnp.dot(l_ref[j], e2_ref[...], preferred_element_type=jnp.float32)
        out_ref[:, place] = (spread + lower_ref[:, place]).astype(jnp.bfloat16)
        return carry

    lax.fori_loop(0, TH1 // 2, columns, 0)


def weight_sums(w_ref, extra_ref, column, imag_column, slots, group):
    targets = w_ref.shape[0]

    def one(b, carry):
        for first in range(slots.start, slots.stop, group):
            rows = slice(first, first + group)
            real = w_ref[b, rows, pl.ds(column, LANES)]
            imag = w_ref[b, rows, pl.ds(imag_column, LANES)]
            extra_ref[b, 0, rows, :] = real + imag
            extra_ref[b, 1, rows, :] = imag - real
        return carry

    lax.fori_loop(0, targets, one, 0, unroll=4)


def mix(w_ref, extra_ref, target, first, column, sources):
    sums = [None] * 3
    for i, (real, imag, both) in enumerate(sources):
        rows = slice(first + i, first + i + 1)
        factors = (
            w_ref[target, rows, pl.ds(column, LANES)],
            extra_ref[target, 0, rows, :],
            extra_ref[target, 1, rows, :],
        )
        for n, (factor, value) in enumerate(zip(factors, (both, imag, real))):
            term = jnp.broadcast_to(factor, value.shape) * value
            sums[n] = term if sums[n] is None else sums[n] + term
    return sums[0] - sums[1], sums[0] + sums[2]


def lower_kernel(rhs, dirs, w_ref, *refs):
    ins, out_ref, extra_ref = refs[:dirs], refs[dirs], refs[dirs + 1]
    width = out_ref.shape[1]
    boxes, slots = w_ref.shape[:2]
    each = slots // dirs
    group = 8

    def columns(j, carry):
        place = rows_of(j, LANES)
        column = pl.multiple_of(j * LANES, LANES)
        weight_sums(w_ref, extra_ref, column, column + width, range(slots), group)
        for base in range(0, slots, group):
            sources = []
            for slot in range(base, base + group):
                row = slot % each * 2 * rhs
                block = ins[slot // each][row : row + 2 * rhs, place].astype(jnp.float32)
                real, imag = block[:rhs], block[rhs:]
                sources.append((real, imag, real + imag))

            def one_box(b, inner):
                real, imag = mix(w_ref, extra_ref, b, base, column, sources)
                both = jnp.concatenate([real, imag], axis=0)
                rows = rows_of(b, 2 * rhs)
                if base:
                    both = both + out_ref[rows, place]
                out_ref[rows, place] = both
                return inner

            lax.fori_loop(0, boxes, one_box, 0, unroll=4)
        return carry

    lax.fori_loop(0, width // LANES, columns, 0)


def parent_kernel(rhs, first_slot, last, n_in, w_ref, *refs):
    ins, refs = refs[:n_in], refs[n_in:]
    before = None
    if last:
        before, refs = refs[0], refs[1:]
    outs, (extra_ref, acc_ref) = refs[:-2], refs[-2:]
    targets = w_ref.shape[0]
    group = ins[0].shape[0]
    rows = ins[0].shape[1] // rhs
    slots = range(first_slot, first_slot + n_in * group)

    def two_rows(j, carry):
        place = rows_of(j, 2 * rhs)
        for step in range(2):
            column = pl.multiple_of((j * 2 + step) * LANES, LANES)
            weight_sums(w_ref, extra_ref, column, column + rows * LANES, slots, group)
            for n in range(n_in):
                sources = []
                for i in range(group):
                    block = ins[n][i, place, :].astype(jnp.float32)
                    block = block[step * rhs : (step + 1) * rhs]
                    real, imag = block[:, :LANES], block[:, LANES:]
                    sources.append((real, imag, real + imag))

                def one_target(q, inner):
                    slot = first_slot + n * group
                    real, imag = mix(w_ref, extra_ref, q, slot, column, sources)
                    if n:
                        real = real + acc_ref[q, step, :, :LANES]
                        imag = imag + acc_ref[q, step, :, LANES:]
                    acc_ref[q, step, :, :LANES] = real
                    acc_ref[q, step, :, LANES:] = imag
                    return inner

                lax.fori_loop(0, targets, one_target, 0, unroll=4)

        each = targets // len(outs)
        for q in range(targets):
            both = jnp.concatenate([acc_ref[q, 0], acc_ref[q, 1]], axis=0)
            if last:
                both = both + before[q, place, :]
            out_ref = outs[q // each]
            out_ref[q % each, place, :] = both.astype(out_ref.dtype)
        return carry

    lax.fori_loop(0, rows // 2, two_rows, 0)


def pair_weights(source_index, kind_index, lengths, slots, axis, table):
    targets = source_index.shape[0]
    kinds, width = table.shape
    return vmem_call(
        functools.partial(weights_kernel, slots, axis, slots // lax.axis_size(axis)),
        jax.ShapeDtypeStruct((targets, slots, width), jnp.float32),
        [pltpu.VMEM((targets * slots, kinds), jnp.bfloat16)],
        3,
        1,
    )(lengths, source_index, kind_index, table)


def swap(value, axis, step):
    count = lax.axis_size(axis)
    return lax.ppermute(value, axis, [(i, i ^ step) for i in range(count)])


def body(
    child_out,
    low_trans,
    up_trans,
    far_src,
    far_kind,
    far_len,
    send_sel,
    par_src,
    par_kind,
    par_len,
    par_sel,
):
    boxes_here, _, rhs, width = child_out.shape
    parents = boxes_here // 8
    dirs, groups = lax.axis_size("dir"), lax.axis_size("grp")
    kinds = low_trans.shape[0]
    rows_here = TH2 // dirs
    tall = 2 * PH2
    slab = (rows_here * rhs, tall)

    rows_up, cols_up = interp_matrix(TH2, TH1), interp_matrix(PH2, PH1)
    scale = TH1 / TH2 * (PH1 / PH2)
    bf = lambda a: jnp.asarray(a.astype(np.float32)).astype(jnp.bfloat16)
    e1 = bf(np.kron(np.eye(2), cols_up.T))
    k1 = bf(np.kron(rows_up, np.eye(rhs)))
    e2 = bf(np.kron(np.eye(2), cols_up) * scale)
    k2 = bf(np.kron(rows_up.T, np.eye(rhs)))
    cosine, sine = phase_tables()
    cosine, sine = jnp.asarray(cosine), jnp.asarray(sine)

    cap = send_sel.shape[3]
    low_slots = dirs * cap
    leaving = vmem_call(
        select_kernel,
        [jax.ShapeDtypeStruct((cap,) + child_out.shape[1:], child_out.dtype)] * dirs,
        [],
        1,
        1,
    )(send_sel.reshape(dirs, cap), child_out)
    early = tuple(range(1, dirs // 2))
    arrived = {0: leaving[0]}
    for k in early:
        arrived[k] = swap(leaving[k], "dir", k)

    flat = child_out.reshape(boxes_here * 2 * rhs, width)
    parent_out = vmem_call(
        functools.partial(aggregate_kernel, rhs, parents, dirs),
        jax.ShapeDtypeStruct((dirs, parents) + slab, jnp.bfloat16),
        [
            pltpu.VMEM((parents, 4, 2, TH1 * rhs, tall), jnp.bfloat16),
            pltpu.VMEM((TH2 * rhs, tall), jnp.float32),
        ],
        5,
    )(flat, e1, k1, cosine, sine)
    sliced = lax.all_to_all(parent_out, "dir", split_axis=0, concat_axis=0, tiled=True)

    offers = par_sel.shape[2]
    up_slots = groups * offers
    up_weights = pair_weights(
        par_src, par_kind, par_len, up_slots, "grp", up_trans.reshape(kinds, -1)
    )
    targets = par_src.shape[0]
    low_weights = pair_weights(
        far_src, far_kind, far_len, low_slots, "dir", low_trans.reshape(kinds, -1)
    )
    sliced, up_weights = lax.optimization_barrier((sliced, up_weights))

    offered = vmem_call(
        offer_kernel, [jax.ShapeDtypeStruct((offers,) + slab, jnp.bfloat16)] * groups, [], 1, 1
    )(par_sel, sliced.reshape((dirs * parents,) + slab))
    late = [k for k in range(1, dirs) if k not in early]
    held = [leaving[k] for k in late]
    offered, held = lax.optimization_barrier((offered, held))
    candidates = [offered[0]]
    for k in range(1, groups):
        candidates.append(swap(offered[k], "grp", k))
    for k, block in zip(late, held):
        arrived[k] = swap(block, "dir", k)

    near = groups // 2
    partial_shape = jax.ShapeDtypeStruct((targets,) + slab, jnp.float32)
    scratch = [
        pltpu.VMEM((targets, 2, up_slots, LANES), jnp.float32),
        pltpu.VMEM((targets, 2, rhs, tall), jnp.float32),
    ]
    started = vmem_call(
        functools.partial(parent_kernel, rhs, 0, False, near), [partial_shape], scratch, 1 + near
    )(up_weights, *candidates[:near])
    parent_in = vmem_call(
        functools.partial(parent_kernel, rhs, near * offers, True, groups - near),
        [jax.ShapeDtypeStruct((targets,) + slab, jnp.bfloat16)],
        scratch,
        2 + groups - near,
    )(up_weights, *candidates[near:], *started)
    parent_in = parent_in[0].reshape((dirs, parents) + slab)
    returned = lax.all_to_all(parent_in, "dir", split_axis=0, concat_axis=0, tiled=True)

    shape = (cap * 2 * rhs, width)
    lower = vmem_call(
        functools.partial(lower_kernel, rhs, dirs),
        jax.ShapeDtypeStruct((boxes_here * 2 * rhs, width), jnp.float32),
        [pltpu.VMEM((boxes_here, 2, low_slots, LANES), jnp.float32)],
        1 + dirs,
    )(low_weights, *[arrived[k].reshape(shape) for k in range(dirs)])

    out = vmem_call(
        functools.partial(disaggregate_kernel, rhs),
        jax.ShapeDtypeStruct((boxes_here * 2 * rhs, width), jnp.bfloat16),
        [
            pltpu.VMEM((parents, TH2 * rhs, tall), jnp.float32),
            pltpu.VMEM((2, TH2 * rhs, tall), jnp.bfloat16),
            pltpu.VMEM((TH1 // 2, boxes_here * 2 * rhs, tall), jnp.bfloat16),
        ],
        6,
    )(returned, lower, e2, k2, cosine, sine)
    return out.reshape(child_out.shape)


def solution(mesh):
    in_specs = (
        P(("grp", "dir"), None, None, None),
        P(),
        P(None, None, "dir", None),
        P(("grp", "dir"), None),
        P(("grp", "dir"), None),
        P(("grp", "dir")),
        P("grp", "dir", None, None),
        P("grp", None),
        P("grp", None),
        P("grp"),
        P(),
    )
    out_specs = P(("grp", "dir"), None, None, None)

    return jax.shard_map(body, mesh=mesh, in_specs=in_specs, out_specs=out_specs, check_vma=False)
```

time: 121 us -> 101 us (0.83)
  the two profiles are of different devices: /device:TPU:0 before, /device:TPU:8 now
where the time goes in v1:
time: 101 us
  Pallas kernels  32 us (32%)
  waiting for transfers between devices  25.6 us (25%)
  starting transfers between devices  25 us (25%)
  local copies, waits for them, and re-layouts  17.7 us (18%)
    ppermute x10, waiting for transfers between devices, swap(): return lax.ppermute(value, axis, [(i, i ^ step) for i in range(count)])  22.4 us
    unnamed x62, local copies, waits for them, and re-layouts  17.6 us
    ppermute x10, starting transfers between devices, swap(): return lax.ppermute(value, axis, [(i, i ^ step) for i in range(count)])  13.9 us
    pallas_call x2, Pallas kernels, pair_weights(): vmem_call(functools.partial(weights_kernel, slots, axis, slots // lax.axi...  8.12 us
    all_to_all x1, starting transfers between devices, body(): lax.all_to_all(parent_out, 'dir', split_axis=0, concat_axis=0, tiled=True)  6.28 us
    pallas_call x1, Pallas kernels, body(): vmem_call(functools.partial(disaggregate_kernel, rhs), jax.ShapeDtypeStru...  5.82 us
    pallas_call x1, Pallas kernels, body(): vmem_call(functools.partial(lower_kernel, rhs, dirs), jax.ShapeDtypeStruc...  5.4 us
    pallas_call x1, Pallas kernels, body(): vmem_call(functools.partial(aggregate_kernel, rhs, parents, dirs), jax.Sh...  5.03 us
  transfers between devices with their start and end apart: 12, of which 8 were waited for; matrix products, arithmetic and copies ran while one was open for 5% of the time, Pallas kernels for 17%

profile of v1, /device:TPU:8, one launch (start us, length us, event | category | flops | bytes accessed | tf_op | source)
XLA Modules:
  0.0 100.7 jit_solution(11767274475733806703)
XLA Ops:
  0.0 1.2 %copy-done.2 = bf16[16,2,8,2048]{3,2,1,0:T(8,128)(2,1)S(1)} copy-done((bf16[16,2,8,2048]{3,2,1,0:T(8,128)(2,1)S(1)}, bf16[16,2,8,2048]{3,2,1,0:T(8,128)(2,1)}, u32[]{:S(2)}) %copy-start.2) | copy-done | bytes 1048600
  1.2 0.9 copy-done.4
  2.1 0.9 copy-done.6
  3.0 0.9 copy-done.9
  4.0 0.8 copy-done.11
  4.8 5.0 %shard_map.163 = bf16[8,2,64,256]{3,2,1,0:T(8,128)(2,1)} custom-call(bf16[256,2048]{1,0:T(8,128)(2,1)S(1)} %bitcast.22, bf16[128,256]{1,0:T(8,128)(2,1)S(1)} %copy-done.11, bf16[512,256]{1,0:T(8,128)(2,1)S(1)} %copy-done.9, f32[4,64,128]{2,1,0:T(8,128)S(1)} %copy-done.4, f32[4,64,128]{2,1,0:T(8,128)S(1)} %copy-done.6), custom_call_target="tpu_custom_call" | custom-call | tf_op jit(solution)/shard_map/pallas_call | solution.py:384
  9.9 6.3 %all-to-all-start = ((bf16[8,2,64,256]{3,2,1,0:T(8,128)(2,1)}), bf16[8,2,64,256]{3,2,1,0:T(8,128)(2,1)S(1)}, u32[]{:S(2)}, u32[]{:S(2)}) async-start(bf16[8,2,64,256]{3,2,1,0:T(8,128)(2,1)} %shard_map.163), calls=%async_computation | async-start | bytes 1048576 | tf_op jit(solution)/shard_map/all_to_all | solution.py:393
  20.7 3.4 %shard_map.164.w_ref = f32[16,32,2048]{2,1,0:T(8,128)S(1)} custom-call(s32[16]{0:T(128)S(1)} %copy-done.17, s32[16,96]{1,0:T(8,128)S(1)} %copy-done.12, s32[16,96]{1,0:T(8,128)S(1)} %copy-done.13, bf16[316,2048]{1,0:T(8,128)(2,1)S(1)} %bitcast.21), custom_call_target="tpu_custom_call" | custom-call | tf_op jit(solution)/shard_map/pallas_call | solution.py:324
  24.2 2.0 %copy-done = f32[16,32,2048]{2,1,0:T(8,128)} copy-done((f32[16,32,2048]{2,1,0:T(8,128)}, f32[16,32,2048]{2,1,0:T(8,128)S(1)}, u32[]{:S(2)}) %copy-start) | copy-done | bytes 4194328
  26.2 3.2 %all-to-all-done = bf16[8,2,64,256]{3,2,1,0:T(8,128)(2,1)S(1)} async-done(((bf16[8,2,64,256]{3,2,1,0:T(8,128)(2,1)}), bf16[8,2,64,256]{3,2,1,0:T(8,128)(2,1)S(1)}, u32[]{:S(2)}, u32[]{:S(2)}) %all-to-all-start) | async-done | bytes 524320 | tf_op jit(solution)/shard_map/all_to_all | solution.py:393
  30.2 1.5 %collective-permute-start = (bf16[8,64,256]{2,1,0:T(8,128)(2,1)S(1)}, bf16[8,64,256]{2,1,0:T(8,128)(2,1)S(1)}, u32[]{:S(2)}, u32[]{:S(2)}) collective-permute-start(bf16[8,64,256]{2,1,0:T(8,128)(2,1)S(1)} %get-tuple-element.37), channel_id=1, source_target_pairs={{0,16},{8,24},{16,0},{24,8},{1,17},{9,25},{17,1},{25,9},{2,18},{10... | collective-permute-start | bytes 786440 | tf_op jit(solution)/shard_map/ppermute | solution.py:335
  32.1 2.2 %copy-done.1 = f32[16,32,2048]{2,1,0:T(8,128)S(1)} copy-done((f32[16,32,2048]{2,1,0:T(8,128)S(1)}, f32[16,32,2048]{2,1,0:T(8,128)}, u32[]{:S(2)}) %copy-start.1) | copy-done | bytes 4194328
  34.3 2.7 %shard_map.167.refs_2_ = f32[16,64,256]{2,1,0:T(8,128)S(1)} custom-call(f32[16,32,2048]{2,1,0:T(8,128)S(1)} %copy-done.1, bf16[8,64,256]{2,1,0:T(8,128)(2,1)S(1)} %get-tuple-element.39.refs_0_, bf16[8,64,256]{2,1,0:T(8,128)(2,1)S(1)} %collective-permute-done.2.refs_1_), custom_call_target="tpu_custom_call" | custom-call | tf_op jit(solution)/shard_map/pallas_call | solution.py:424
  37.0 2.5 %collective-permute-done.refs_0_ = bf16[8,64,256]{2,1,0:T(8,128)(2,1)S(1)} collective-permute-done((bf16[8,64,256]{2,1,0:T(8,128)(2,1)S(1)}, bf16[8,64,256]{2,1,0:T(8,128)(2,1)S(1)}, u32[]{:S(2)}, u32[]{:S(2)}) %collective-permute-start) | collective-permute-done | bytes 262176 | tf_op jit(solution)/shard_map/ppermute | solution.py:335
  39.5 4.5 %collective-permute-done.1.refs_1_ = bf16[8,64,256]{2,1,0:T(8,128)(2,1)S(1)} collective-permute-done((bf16[8,64,256]{2,1,0:T(8,128)(2,1)S(1)}, bf16[8,64,256]{2,1,0:T(8,128)(2,1)S(1)}, u32[]{:S(2)}, u32[]{:S(2)}) %collective-permute-start.1) | collective-permute-done | bytes 262176 | tf_op jit(solution)/shard_map/ppermute | solution.py:335
  44.0 3.5 %shard_map.168 = bf16[16,64,256]{2,1,0:T(8,128)(2,1)} custom-call(f32[16,32,2048]{2,1,0:T(8,128)S(1)} %copy-done.1, bf16[8,64,256]{2,1,0:T(8,128)(2,1)S(1)} %collective-permute-done.refs_0_, bf16[8,64,256]{2,1,0:T(8,128)(2,1)S(1)} %collective-permute-done.1.refs_1_, f32[16,64,256]{2,1,0:T(8,128)S(1)} %shard_map.167.refs_2_), custom_call_target="tpu_custom_call" | custom-call | tf_op jit(solution)/shard_map/pallas_call | solution.py:427
  47.5 4.9 %all-to-all-start.1 = ((bf16[8,2,64,256]{3,2,1,0:T(8,128)(2,1)}), bf16[8,2,64,256]{3,2,1,0:T(8,128)(2,1)S(1)}, u32[]{:S(2)}, u32[]{:S(2)}) async-start(bf16[8,2,64,256]{3,2,1,0:T(8,128)(2,1)} %bitcast.3), calls=%async_computation.1 | async-start | bytes 1048576 | tf_op jit(solution)/shard_map/all_to_all | solution.py:434
  52.4 1.5 %collective-permute-start.3 = (bf16[2,2,8,2048]{3,2,1,0:T(8,128)(2,1)S(1)}, bf16[2,2,8,2048]{3,2,1,0:T(8,128)(2,1)S(1)}, u32[]{:S(2)}, u32[]{:S(2)}) collective-permute-start(bf16[2,2,8,2048]{3,2,1,0:T(8,128)(2,1)S(1)} %copy-done.26), channel_id=1, source_target_pairs={{0,1},{1,0},{2,3},{3,2},{4,5},{5,4},{6,7},{7,6},{8,9},{9,8},{10,11... | collective-permute-start | bytes 393224 | tf_op jit(solution)/shard_map/ppermute | solution.py:335
  54.4 1.5 %collective-permute-start.5 = (bf16[2,2,8,2048]{3,2,1,0:T(8,128)(2,1)S(1)}, bf16[2,2,8,2048]{3,2,1,0:T(8,128)(2,1)S(1)}, u32[]{:S(2)}, u32[]{:S(2)}) collective-permute-start(bf16[2,2,8,2048]{3,2,1,0:T(8,128)(2,1)S(1)} %copy-done.22), channel_id=1, source_target_pairs={{0,3},{1,2},{2,1},{3,0},{4,7},{5,6},{6,5},{7,4},{8,11},{9,10},{10,... | collective-permute-start | bytes 393224 | tf_op jit(solution)/shard_map/ppermute | solution.py:335
  55.9 2.4 %collective-permute-start.6 = (bf16[2,2,8,2048]{3,2,1,0:T(8,128)(2,1)S(1)}, bf16[2,2,8,2048]{3,2,1,0:T(8,128)(2,1)S(1)}, u32[]{:S(2)}, u32[]{:S(2)}) collective-permute-start(bf16[2,2,8,2048]{3,2,1,0:T(8,128)(2,1)S(1)} %copy-done.20), channel_id=1, source_target_pairs={{0,4},{1,5},{2,6},{3,7},{4,0},{5,1},{6,2},{7,3},{8,12},{9,13},{10,... | collective-permute-start | bytes 393224 | tf_op jit(solution)/shard_map/ppermute | solution.py:335
  58.3 1.5 %collective-permute-start.7 = (bf16[2,2,8,2048]{3,2,1,0:T(8,128)(2,1)S(1)}, bf16[2,2,8,2048]{3,2,1,0:T(8,128)(2,1)S(1)}, u32[]{:S(2)}, u32[]{:S(2)}) collective-permute-start(bf16[2,2,8,2048]{3,2,1,0:T(8,128)(2,1)S(1)} %get-tuple-element.46), channel_id=1, source_target_pairs={{0,5},{1,4},{2,7},{3,6},{4,1},{5,0},{6,3},{7,2},{8,13},{9,12},{10,... | collective-permute-start | bytes 393224 | tf_op jit(solution)/shard_map/ppermute | solution.py:335
  59.7 2.5 %collective-permute-done.3 = bf16[2,2,8,2048]{3,2,1,0:T(8,128)(2,1)S(1)} collective-permute-done((bf16[2,2,8,2048]{3,2,1,0:T(8,128)(2,1)S(1)}, bf16[2,2,8,2048]{3,2,1,0:T(8,128)(2,1)S(1)}, u32[]{:S(2)}, u32[]{:S(2)}) %collective-permute-start.3) | collective-permute-done | bytes 131104 | tf_op jit(solution)/shard_map/ppermute | solution.py:335
  62.9 2.5 %collective-permute-done.4 = bf16[2,2,8,2048]{3,2,1,0:T(8,128)(2,1)S(1)} collective-permute-done((bf16[2,2,8,2048]{3,2,1,0:T(8,128)(2,1)S(1)}, bf16[2,2,8,2048]{3,2,1,0:T(8,128)(2,1)S(1)}, u32[]{:S(2)}, u32[]{:S(2)}) %collective-permute-start.4) | collective-permute-done | bytes 131104 | tf_op jit(solution)/shard_map/ppermute | solution.py:335
  65.4 4.0 %collective-permute-start.9 = (bf16[2,2,8,2048]{3,2,1,0:T(8,128)(2,1)S(1)}, bf16[2,2,8,2048]{3,2,1,0:T(8,128)(2,1)S(1)}, u32[]{:S(2)}, u32[]{:S(2)}) collective-permute-start(bf16[2,2,8,2048]{3,2,1,0:T(8,128)(2,1)S(1)} %get-tuple-element.48), channel_id=1, source_target_pairs={{0,7},{1,6},{2,5},{3,4},{4,3},{5,2},{6,1},{7,0},{8,15},{9,14},{10,... | collective-permute-start | bytes 393224 | tf_op jit(solution)/shard_map/ppermute | solution.py:335
  69.4 3.7 %pad.1 = bf16[320,2,2048]{2,1,0:T(2,128)(2,1)S(1)} pad(bf16[316,2,2048]{2,1,0:T(2,128)(2,1)} %param.18, bf16[]{:T(256)} %constant.27), padding=0_4x0_0x0_0 | pad | bytes 5210114
  73.2 1.1 %copy.20 = bf16[40,8,2,2048]{3,1,2,0:T(8,128)(2,1)S(1)} copy(bf16[40,8,2,2048]{3,2,1,0:T(2,128)(2,1)S(1)} %bitcast.32) | data formatting | bytes 5242880
  74.3 4.7 %shard_map.169.w_ref = f32[16,16,4096]{2,1,0:T(8,128)S(1)} custom-call(s32[16]{0:T(128)S(1)} %copy-done.18, s32[16,96]{1,0:T(8,128)S(1)} %copy-done.15, s32[16,96]{1,0:T(8,128)S(1)} %copy-done.16, bf16[316,4096]{1,0:T(8,128)(2,1)S(1)} %bitcast.20), custom_call_target="tpu_custom_call" | custom-call | tf_op jit(solution)/shard_map/pallas_call | solution.py:324
  79.0 1.8 %collective-permute-done.7 = bf16[2,2,8,2048]{3,2,1,0:T(8,128)(2,1)S(1)} collective-permute-done((bf16[2,2,8,2048]{3,2,1,0:T(8,128)(2,1)S(1)}, bf16[2,2,8,2048]{3,2,1,0:T(8,128)(2,1)S(1)}, u32[]{:S(2)}, u32[]{:S(2)}) %collective-permute-start.7) | collective-permute-done | bytes 131104 | tf_op jit(solution)/shard_map/ppermute | solution.py:335
  80.9 5.7 %collective-permute-done.8 = bf16[2,2,8,2048]{3,2,1,0:T(8,128)(2,1)S(1)} collective-permute-done((bf16[2,2,8,2048]{3,2,1,0:T(8,128)(2,1)S(1)}, bf16[2,2,8,2048]{3,2,1,0:T(8,128)(2,1)S(1)}, u32[]{:S(2)}, u32[]{:S(2)}) %collective-permute-start.8) | collective-permute-done | bytes 131104 | tf_op jit(solution)/shard_map/ppermute | solution.py:335
  86.6 2.8 %collective-permute-done.9 = bf16[2,2,8,2048]{3,2,1,0:T(8,128)(2,1)S(1)} collective-permute-done((bf16[2,2,8,2048]{3,2,1,0:T(8,128)(2,1)S(1)}, bf16[2,2,8,2048]{3,2,1,0:T(8,128)(2,1)S(1)}, u32[]{:S(2)}, u32[]{:S(2)}) %collective-permute-start.9) | collective-permute-done | bytes 131104 | tf_op jit(solution)/shard_map/ppermute | solution.py:335
  89.4 5.4 %shard_map.170.lower_ref = f32[256,2048]{1,0:T(8,128)S(1)} custom-call(f32[16,16,4096]{2,1,0:T(8,128)S(1)} %shard_map.169.w_ref, bf16[32,2048]{1,0:T(8,128)(2,1)S(1)} %bitcast.24, bf16[32,2048]{1,0:T(8,128)(2,1)S(1)} %bitcast.25, bf16[32,2048]{1,0:T(8,128)(2,1)S(1)} %bitcast.26, bf16[32,2048]{1,0:T(8,128)(2,1)S(1)} %bitcast.27, ...), custom_call_target="tpu_custom_call" | custom-call | tf_op jit(solution)/shard_map/pallas_call | solution.py:437
  94.9 5.8 %shard_map.171 = bf16[256,2048]{1,0:T(8,128)(2,1)} custom-call(bf16[8,2,64,256]{3,2,1,0:T(8,128)(2,1)S(1)} %all-to-all-done.1.in_ref, f32[256,2048]{1,0:T(8,128)S(1)} %shard_map.170.lower_ref, bf16[256,128]{1,0:T(8,128)(2,1)S(1)} %copy-done.10, bf16[256,512]{1,0:T(8,128)(2,1)S(1)} %copy-done.8, f32[4,64,128]{2,1,0:T(8,128)S(1)} %copy-done.5, ...), custom_call_target="tpu_custom_call" | custom-call | tf_op jit(solution)/shard_map/pallas_call | solution.py:444
  (64 shorter events, 6.9 us)
Async XLA Ops:
  0.0 1.2 %copy-start.2 = (bf16[16,2,8,2048]{3,2,1,0:T(8,128)(2,1)S(1)}, bf16[16,2,8,2048]{3,2,1,0:T(8,128)(2,1)}, u32[]{:S(2)}) copy-start(bf16[16,2,8,2048]{3,2,1,0:T(8,128)(2,1)} %x_ref.1) | copy-start | bytes 3145732
  4.8 11.3 %copy-start.27 = (bf16[316,2,8,128]{3,2,1,0:T(8,128)(2,1)S(1)}, bf16[316,2,8,128]{3,2,1,0:T(8,128)(2,1)}, u32[]{:S(2)}) copy-start(bf16[316,2,8,128]{3,2,1,0:T(8,128)(2,1)} %param.19) | copy-start | bytes 3883012
  9.9 19.5 %all-to-all-start = ((bf16[8,2,64,256]{3,2,1,0:T(8,128)(2,1)}), bf16[8,2,64,256]{3,2,1,0:T(8,128)(2,1)S(1)}, u32[]{:S(2)}, u32[]{:S(2)}) async-start(bf16[8,2,64,256]{3,2,1,0:T(8,128)(2,1)} %shard_map.163), calls=%async_computation | async-start | bytes 1048576 | tf_op jit(solution)/shard_map/all_to_all | solution.py:393
  16.1 1.2 %copy-start.3 = (bf16[16,2,8,2048]{3,2,1,0:T(8,128)(2,1)S(1)}, bf16[16,2,8,2048]{3,2,1,0:T(8,128)(2,1)}, u32[]{:S(2)}) copy-start(bf16[16,2,8,2048]{3,2,1,0:T(8,128)(2,1)} %x_ref.1) | copy-start | bytes 3145732
  16.2 4.6 %copy-start.12 = (s32[16,96]{1,0:T(8,128)S(1)}, s32[16,96]{1,0:T(8,128)}, u32[]{:S(2)}) copy-start(s32[16,96]{1,0:T(8,128)} %source_ref.2) | copy-start | bytes 18436
  16.2 4.6 %copy-start.13 = (s32[16,96]{1,0:T(8,128)S(1)}, s32[16,96]{1,0:T(8,128)}, u32[]{:S(2)}) copy-start(s32[16,96]{1,0:T(8,128)} %kind_ref.2) | copy-start | bytes 18436
  16.2 4.6 %copy-start.17 = (s32[16]{0:T(128)S(1)}, s32[16]{0:T(128)}, u32[]{:S(2)}) copy-start(s32[16]{0:T(128)} %length_ref.2) | copy-start | bytes 196
  20.7 8.6 %copy-start.14 = (s32[4,4,8]{2,1,0:T(4,128)S(1)}, s32[4,4,8]{2,1,0:T(4,128)}, u32[]{:S(2)}) copy-start(s32[4,4,8]{2,1,0:T(4,128)} %pick_ref.1) | copy-start | bytes 1540
  24.2 2.0 %copy-start = (f32[16,32,2048]{2,1,0:T(8,128)}, f32[16,32,2048]{2,1,0:T(8,128)S(1)}, u32[]{:S(2)}) copy-start(f32[16,32,2048]{2,1,0:T(8,128)S(1)} %shard_map.164.w_ref) | copy-start | bytes 12582916
  30.1 1.9 %collective-permute-start.2 = (bf16[8,64,256]{2,1,0:T(8,128)(2,1)S(1)}, bf16[8,64,256]{2,1,0:T(8,128)(2,1)S(1)}, u32[]{:S(2)}, u32[]{:S(2)}) collective-permute-start(bf16[8,64,256]{2,1,0:T(8,128)(2,1)S(1)} %get-tuple-element.40), channel_id=1, source_target_pairs={{0,8},{8,0},{16,24},{24,16},{1,9},{9,1},{17,25},{25,17},{2,10},{10... | collective-permute-start | bytes 786440 | tf_op jit(solution)/shard_map/ppermute | solution.py:335
  30.2 9.2 %collective-permute-start = (bf16[8,64,256]{2,1,0:T(8,128)(2,1)S(1)}, bf16[8,64,256]{2,1,0:T(8,128)(2,1)S(1)}, u32[]{:S(2)}, u32[]{:S(2)}) collective-permute-start(bf16[8,64,256]{2,1,0:T(8,128)(2,1)S(1)} %get-tuple-element.37), channel_id=1, source_target_pairs={{0,16},{8,24},{16,0},{24,8},{1,17},{9,25},{17,1},{25,9},{2,18},{10... | collective-permute-start | bytes 786440 | tf_op jit(solution)/shard_map/ppermute | solution.py:335
  31.8 12.2 %collective-permute-start.1 = (bf16[8,64,256]{2,1,0:T(8,128)(2,1)S(1)}, bf16[8,64,256]{2,1,0:T(8,128)(2,1)S(1)}, u32[]{:S(2)}, u32[]{:S(2)}) collective-permute-start(bf16[8,64,256]{2,1,0:T(8,128)(2,1)S(1)} %get-tuple-element.38), channel_id=1, source_target_pairs={{0,24},{8,16},{16,8},{24,0},{1,25},{9,17},{17,9},{25,1},{2,26},{10... | collective-permute-start | bytes 786440 | tf_op jit(solution)/shard_map/ppermute | solution.py:335
  32.1 2.2 %copy-start.1 = (f32[16,32,2048]{2,1,0:T(8,128)S(1)}, f32[16,32,2048]{2,1,0:T(8,128)}, u32[]{:S(2)}) copy-start(f32[16,32,2048]{2,1,0:T(8,128)} %copy-done) | copy-start | bytes 12582916
  37.0 15.5 %copy-start.26 = (bf16[2,2,8,2048]{3,2,1,0:T(8,128)(2,1)S(1)}, bf16[2,2,8,2048]{3,2,1,0:T(8,128)(2,1)}, u32[]{:S(2)}) copy-start(bf16[2,2,8,2048]{3,2,1,0:T(8,128)(2,1)} %copy-done.25) | copy-start | bytes 393220
  37.0 16.9 %copy-start.24 = (bf16[2,2,8,2048]{3,2,1,0:T(8,128)(2,1)S(1)}, bf16[2,2,8,2048]{3,2,1,0:T(8,128)(2,1)}, u32[]{:S(2)}) copy-start(bf16[2,2,8,2048]{3,2,1,0:T(8,128)(2,1)} %copy-done.23) | copy-start | bytes 393220
  37.0 17.5 %copy-start.22 = (bf16[2,2,8,2048]{3,2,1,0:T(8,128)(2,1)S(1)}, bf16[2,2,8,2048]{3,2,1,0:T(8,128)(2,1)}, u32[]{:S(2)}) copy-start(bf16[2,2,8,2048]{3,2,1,0:T(8,128)(2,1)} %copy-done.21) | copy-start | bytes 393220
  37.0 18.9 %copy-start.20 = (bf16[2,2,8,2048]{3,2,1,0:T(8,128)(2,1)S(1)}, bf16[2,2,8,2048]{3,2,1,0:T(8,128)(2,1)}, u32[]{:S(2)}) copy-start(bf16[2,2,8,2048]{3,2,1,0:T(8,128)(2,1)} %copy-done.19) | copy-start | bytes 393220
  47.5 47.3 %all-to-all-start.1 = ((bf16[8,2,64,256]{3,2,1,0:T(8,128)(2,1)}), bf16[8,2,64,256]{3,2,1,0:T(8,128)(2,1)S(1)}, u32[]{:S(2)}, u32[]{:S(2)}) async-start(bf16[8,2,64,256]{3,2,1,0:T(8,128)(2,1)} %bitcast.3), calls=%async_computation.1 | async-start | bytes 1048576 | tf_op jit(solution)/shard_map/all_to_all | solution.py:434
  52.4 9.9 %collective-permute-start.3 = (bf16[2,2,8,2048]{3,2,1,0:T(8,128)(2,1)S(1)}, bf16[2,2,8,2048]{3,2,1,0:T(8,128)(2,1)S(1)}, u32[]{:S(2)}, u32[]{:S(2)}) collective-permute-start(bf16[2,2,8,2048]{3,2,1,0:T(8,128)(2,1)S(1)} %copy-done.26), channel_id=1, source_target_pairs={{0,1},{1,0},{2,3},{3,2},{4,5},{5,4},{6,7},{7,6},{8,9},{9,8},{10,11... | collective-permute-start | bytes 393224 | tf_op jit(solution)/shard_map/ppermute | solution.py:335
  53.9 11.5 %collective-permute-start.4 = (bf16[2,2,8,2048]{3,2,1,0:T(8,128)(2,1)S(1)}, bf16[2,2,8,2048]{3,2,1,0:T(8,128)(2,1)S(1)}, u32[]{:S(2)}, u32[]{:S(2)}) collective-permute-start(bf16[2,2,8,2048]{3,2,1,0:T(8,128)(2,1)S(1)} %copy-done.24), channel_id=1, source_target_pairs={{0,2},{1,3},{2,0},{3,1},{4,6},{5,7},{6,4},{7,5},{8,10},{9,11},{10,... | collective-permute-start | bytes 393224 | tf_op jit(solution)/shard_map/ppermute | solution.py:335
  54.4 24.6 %collective-permute-start.5 = (bf16[2,2,8,2048]{3,2,1,0:T(8,128)(2,1)S(1)}, bf16[2,2,8,2048]{3,2,1,0:T(8,128)(2,1)S(1)}, u32[]{:S(2)}, u32[]{:S(2)}) collective-permute-start(bf16[2,2,8,2048]{3,2,1,0:T(8,128)(2,1)S(1)} %copy-done.22), channel_id=1, source_target_pairs={{0,3},{1,2},{2,1},{3,0},{4,7},{5,6},{6,5},{7,4},{8,11},{9,10},{10,... | collective-permute-start | bytes 393224 | tf_op jit(solution)/shard_map/ppermute | solution.py:335
  55.9 23.1 %collective-permute-start.6 = (bf16[2,2,8,2048]{3,2,1,0:T(8,128)(2,1)S(1)}, bf16[2,2,8,2048]{3,2,1,0:T(8,128)(2,1)S(1)}, u32[]{:S(2)}, u32[]{:S(2)}) collective-permute-start(bf16[2,2,8,2048]{3,2,1,0:T(8,128)(2,1)S(1)} %copy-done.20), channel_id=1, source_target_pairs={{0,4},{1,5},{2,6},{3,7},{4,0},{5,1},{6,2},{7,3},{8,12},{9,13},{10,... | collective-permute-start | bytes 393224 | tf_op jit(solution)/shard_map/ppermute | solution.py:335
  58.3 22.6 %collective-permute-start.7 = (bf16[2,2,8,2048]{3,2,1,0:T(8,128)(2,1)S(1)}, bf16[2,2,8,2048]{3,2,1,0:T(8,128)(2,1)S(1)}, u32[]{:S(2)}, u32[]{:S(2)}) collective-permute-start(bf16[2,2,8,2048]{3,2,1,0:T(8,128)(2,1)S(1)} %get-tuple-element.46), channel_id=1, source_target_pairs={{0,5},{1,4},{2,7},{3,6},{4,1},{5,0},{6,3},{7,2},{8,13},{9,12},{10,... | collective-permute-start | bytes 393224 | tf_op jit(solution)/shard_map/ppermute | solution.py:335
  62.3 24.3 %collective-permute-start.8 = (bf16[2,2,8,2048]{3,2,1,0:T(8,128)(2,1)S(1)}, bf16[2,2,8,2048]{3,2,1,0:T(8,128)(2,1)S(1)}, u32[]{:S(2)}, u32[]{:S(2)}) collective-permute-start(bf16[2,2,8,2048]{3,2,1,0:T(8,128)(2,1)S(1)} %get-tuple-element.47), channel_id=1, source_target_pairs={{0,6},{1,7},{2,4},{3,5},{4,2},{5,3},{6,0},{7,1},{8,14},{9,15},{10,... | collective-permute-start | bytes 393224 | tf_op jit(solution)/shard_map/ppermute | solution.py:335
  65.4 24.0 %collective-permute-start.9 = (bf16[2,2,8,2048]{3,2,1,0:T(8,128)(2,1)S(1)}, bf16[2,2,8,2048]{3,2,1,0:T(8,128)(2,1)S(1)}, u32[]{:S(2)}, u32[]{:S(2)}) collective-permute-start(bf16[2,2,8,2048]{3,2,1,0:T(8,128)(2,1)S(1)} %get-tuple-element.48), channel_id=1, source_target_pairs={{0,7},{1,6},{2,5},{3,4},{4,3},{5,2},{6,1},{7,0},{8,15},{9,14},{10,... | collective-permute-start | bytes 393224 | tf_op jit(solution)/shard_map/ppermute | solution.py:335
  73.1 1.2 %copy-start.15 = (s32[16,96]{1,0:T(8,128)S(1)}, s32[16,96]{1,0:T(8,128)}, u32[]{:S(2)}) copy-start(s32[16,96]{1,0:T(8,128)} %source_ref.3) | copy-start | bytes 18436
  73.1 1.2 %copy-start.16 = (s32[16,96]{1,0:T(8,128)S(1)}, s32[16,96]{1,0:T(8,128)}, u32[]{:S(2)}) copy-start(s32[16,96]{1,0:T(8,128)} %kind_ref.3) | copy-start | bytes 18436
  73.2 1.2 %copy-start.18 = (s32[16]{0:T(128)S(1)}, s32[16]{0:T(128)}, u32[]{:S(2)}) copy-start(s32[16]{0:T(128)} %length_ref.3) | copy-start | bytes 196
  89.4 5.4 %copy-start.5 = (f32[4,64,128]{2,1,0:T(8,128)S(1)}, f32[4,64,128]{2,1,0:T(8,128)}, u32[]{:S(2)}) copy-start(f32[4,64,128]{2,1,0:T(8,128)} %constant.16.clone.cos_ref) | copy-start | bytes 393220
  89.4 5.4 %copy-start.7 = (f32[4,64,128]{2,1,0:T(8,128)S(1)}, f32[4,64,128]{2,1,0:T(8,128)}, u32[]{:S(2)}) copy-start(f32[4,64,128]{2,1,0:T(8,128)} %constant.17.clone.sin_ref) | copy-start | bytes 393220
  89.4 5.5 %copy-start.8 = (bf16[256,512]{1,0:T(8,128)(2,1)S(1)}, bf16[256,512]{1,0:T(8,128)(2,1)}, u32[]{:S(2)}) copy-start(bf16[256,512]{1,0:T(8,128)(2,1)} %constant.26.k2_ref) | copy-start | bytes 786436
  89.4 5.5 %copy-start.10 = (bf16[256,128]{1,0:T(8,128)(2,1)S(1)}, bf16[256,128]{1,0:T(8,128)(2,1)}, u32[]{:S(2)}) copy-start(bf16[256,128]{1,0:T(8,128)(2,1)} %constant.25.e2_ref) | copy-start | bytes 196612
  (9 other events, 6.9 us)
